TPU v7x, 256 devices: a whole 4x4x8 slice. The times are simulated.
256 devices in a mesh: dp: 2 (over y_lo), ctx: 16 (over y_hi, z), tensor: 8 (over x, core).
Axes of the slice: x: 4, y: 4 (y_hi: 2, y_lo: 2; y = y_hi * 2 + y_lo), z: 8, core: 2. Of those that a mesh axis runs over, the one named last changes fastest.
Arguments:
- input_spikes: int32 [512, 8192], P(None, ('dp', 'ctx')), may hold values from 0 to 65535
- query_spikes: int32 [512, 8192], P('tensor', ('dp', 'ctx')), may hold values from 0 to 65535
- key_spikes: int32 [512, 8192], P('tensor', ('dp', 'ctx')), may hold values from 0 to 65535
- values: bfloat16 [8192, 8192], P(('dp', 'ctx'), 'tensor'), may hold values from -6 to 6
- query_slope: bfloat16 [8192, 8192], P(('dp', 'ctx'), 'tensor'), may hold values from 0.25 to 2
- key_slope: bfloat16 [8192, 8192], P(('dp', 'ctx'), 'tensor'), may hold values from 0.25 to 2
- grad_out: bfloat16 [8192, 8192], P(('dp', 'ctx'), 'tensor'), may hold values from -6 to 6
- log_gate: float32 [64, 8192], P('tensor', ('dp', 'ctx')), may hold values from -0.8 to 0
- pattern: int32 [128, 16], P('tensor'), may hold values from 0 to 127, all different within a row
Outputs:
- query_grad: bfloat16 [8192, 8192], P(('dp', 'ctx'), 'tensor')
- key_grad: bfloat16 [8192, 8192], P(('dp', 'ctx'), 'tensor')
- value_grad: float32 [16, 128, 4096], P('ctx', 'tensor')
Inputs may be any that keep to these rules, and one draw needn't show every extreme that they name: `pattern`: each column block names 16 different row blocks.
All inputs are finite; a program needn't handle non-finite values.
Results may differ from a plain program's by a relative error of at most 0.0073.
Values sent between devices are 32-bit elements; how exact they have to be, the bound alone decides.
A program may use at most 128 MiB of HBM per device.

v0:
```python
import jax
import jax.numpy as jnp
from jax import lax
from jax.sharding import PartitionSpec as P

D = 8192
HEAD = 128
BLK = 64
SEL = 16
highest = lax.Precision.HIGHEST


def entering(value, axis, combine, identity, reverse):
    devices, place = (lax.axis_size(axis), lax.axis_index(axis))
    everything = jax.tree.map(lambda part: lax.all_gather(part, axis), value)
    start = jax.tree.map(
        lambda part, zero: jnp.broadcast_to(jnp.asarray(zero, part.dtype), part.shape),
        value,
        identity,
    )

    def turn(k, before):
        at = devices - 1 - k if reverse else k
        reached = at > place if reverse else at < place
        new = combine(before, jax.tree.map(lambda part: part[at], everything))
        return jax.tree.map(lambda a, b: jnp.where(reached, a, b), new, before)

    return lax.fori_loop(0, devices, turn, start)


def dims_of(left_dim, right_dim):
    return (((left_dim,), (right_dim,)), ((), ()))


def unpack_flags(packed):
    shifts = jnp.arange(16, dtype=jnp.int32)
    flags = jnp.bitwise_and(jnp.right_shift(packed[:, None, :], shifts[None, :, None]), 1)
    return flags.reshape(packed.shape[0] * 16, packed.shape[1]).astype(jnp.bfloat16)


def decay_matrix(cumulative):
    spread = cumulative[:, None] - cumulative[None, :]
    places = jnp.arange(cumulative.shape[0])
    causal = places[:, None] >= places[None, :]
    return jnp.where(causal, jnp.exp(jnp.minimum(spread, 0.0)), 0.0)


def first_phase(query_cols, key_cols, head_values, cumulative):
    decays = decay_matrix(cumulative)
    intersection = lax.dot_general(
        query_cols, key_cols, dims_of(0, 0), preferred_element_type=jnp.float32
    )
    weights = intersection * decays
    weights_low = weights.astype(jnp.bfloat16)
    local_num = jnp.dot(weights_low, head_values, preferred_element_type=jnp.float32)
    local_den = jnp.sum(weights, axis=1)
    tail_decay = jnp.exp(cumulative[-1] - cumulative)
    key_float = key_cols.astype(jnp.float32) * tail_decay[None, :]
    state_sum = jnp.dot(key_float, head_values.astype(jnp.float32), precision=highest)
    key_sum = jnp.sum(key_float, axis=1)
    return (weights_low, local_num, local_den, jnp.exp(cumulative[-1]), state_sum, key_sum)


def second_phase(
    query_cols,
    key_cols,
    head_values,
    head_grad,
    cumulative,
    weights_low,
    local_num,
    local_den,
    state_in,
    keys_in,
):
    decays = decay_matrix(cumulative)
    lead_decay = jnp.exp(cumulative)
    query_float = query_cols.astype(jnp.float32)
    carried_num = lax.dot_general(query_float, state_in, dims_of(0, 0), precision=highest)
    numerator = local_num + lead_decay[:, None] * carried_num
    denominator = 1.0 + local_den + lead_decay * jnp.dot(keys_in, query_float, precision=highest)
    output = numerator / denominator[:, None]
    grad_float = head_grad.astype(jnp.float32)
    scaled = grad_float / denominator[:, None]
    norm_grad = -jnp.sum(grad_float * output, axis=1) / denominator
    scaled_low = scaled.astype(jnp.bfloat16)
    cross_term = lax.dot_general(
        scaled_low, head_values, dims_of(1, 1), preferred_element_type=jnp.float32
    )
    mixed_low = ((cross_term + norm_grad[:, None]) * decays).astype(jnp.bfloat16)
    carried_query = (
        lax.dot_general(scaled, state_in, dims_of(1, 1), precision=highest)
        + norm_grad[:, None] * keys_in[None, :]
    )
    grad_query = (
        lax.dot_general(mixed_low, key_cols, dims_of(1, 1), preferred_element_type=jnp.float32)
        + lead_decay[:, None] * carried_query
    )
    grad_key = lax.dot_general(
        mixed_low, query_cols, dims_of(0, 1), preferred_element_type=jnp.float32
    )
    grad_value = lax.dot_general(
        weights_low, scaled_low, dims_of(0, 0), preferred_element_type=jnp.float32
    )
    adjoint_sum = jnp.dot(query_float * lead_decay[None, :], scaled, precision=highest)
    adjoint_vec = jnp.dot(query_float, lead_decay * norm_grad, precision=highest)
    return (grad_query, grad_key, grad_value, adjoint_sum, adjoint_vec)


def third_phase(
    key_cols, head_values, cumulative, grad_key_local, grad_value_local, adjoint, adjoint_vec
):
    tail_decay = jnp.exp(cumulative[-1] - cumulative)[:, None]
    value_float = head_values.astype(jnp.float32)
    key_float = key_cols.astype(jnp.float32)
    grad_key = grad_key_local + tail_decay * (
        lax.dot_general(value_float, adjoint, dims_of(1, 1), precision=highest)
        + adjoint_vec[None, :]
    )
    grad_value = grad_value_local + tail_decay * lax.dot_general(
        key_float, adjoint, dims_of(0, 0), precision=highest
    )
    return (grad_key, grad_value)


def combine_forward(earlier_part, later_part):
    total_early, state_early, keys_early = earlier_part
    total_late, state_late, keys_late = later_part
    return (
        total_early * total_late,
        total_late[:, None, None] * state_early + state_late,
        total_late[:, None] * keys_early + keys_late,
    )


def combine_backward(earlier_part, later_part):
    total_early, adjoint_early, vector_early = earlier_part
    total_late, adjoint_late, vector_late = later_part
    return (
        total_early * total_late,
        adjoint_late + total_late[:, None, None] * adjoint_early,
        vector_late + total_late[:, None] * vector_early,
    )


def run_first(block_items):
    return first_phase(*block_items)


def run_second(block_items):
    return second_phase(*block_items)


def per_device(
    input_spikes,
    query_spikes,
    key_spikes,
    values,
    query_slope,
    key_slope,
    grad_out,
    log_gate,
    pattern,
):
    tokens_here = values.shape[0]
    heads_here = values.shape[1] // HEAD
    query_cols = unpack_flags(query_spikes).reshape(heads_here, HEAD, tokens_here)
    key_cols = unpack_flags(key_spikes).reshape(heads_here, HEAD, tokens_here)
    head_values = values.reshape(tokens_here, heads_here, HEAD).transpose(1, 0, 2)
    head_grads = grad_out.reshape(tokens_here, heads_here, HEAD).transpose(1, 0, 2)
    cumulative = jnp.cumsum(log_gate, axis=1)
    weights_low, local_num, local_den, totals, state_sum, key_sum = lax.map(
        run_first, (query_cols, key_cols, head_values, cumulative)
    )
    identity_state = (
        jnp.ones((heads_here,), jnp.float32),
        jnp.zeros((heads_here, HEAD, HEAD), jnp.float32),
        jnp.zeros((heads_here, HEAD), jnp.float32),
    )
    carried_state = entering(
        (totals, state_sum, key_sum), "ctx", combine_forward, identity_state, False
    )
    grad_query, grad_key_local, grad_value_local, adjoint_sum, adjoint_vec = lax.map(
        run_second,
        (
            query_cols,
            key_cols,
            head_values,
            head_grads,
            cumulative,
            weights_low,
            local_num,
            local_den,
            carried_state[1],
            carried_state[2],
        ),
    )
    carried_adjoint = entering(
        (totals, adjoint_sum, adjoint_vec), "ctx", combine_backward, identity_state, True
    )
    grad_key, grad_value = jax.vmap(third_phase)(
        key_cols,
        head_values,
        cumulative,
        grad_key_local,
        grad_value_local,
        carried_adjoint[1],
        carried_adjoint[2],
    )
    width_here = heads_here * HEAD
    flat_query = grad_query.transpose(1, 0, 2).reshape(tokens_here, width_here)
    flat_key = grad_key.transpose(1, 0, 2).reshape(tokens_here, width_here)
    query_grad = (query_slope.astype(jnp.float32) * flat_query).astype(jnp.bfloat16)
    key_grad = (key_slope.astype(jnp.float32) * flat_key).astype(jnp.bfloat16)
    column_blocks = pattern.shape[0]
    value_low = grad_value.transpose(1, 0, 2).reshape(tokens_here, width_here).astype(jnp.bfloat16)
    value_blocks = value_low.reshape(tokens_here, column_blocks, BLK)
    input_cols = unpack_flags(input_spikes)
    row_share = SEL // lax.axis_size("ctx")
    input_blocks = input_cols.reshape(D // BLK, BLK, tokens_here)
    chosen = pattern.T
    gathered = jnp.take(input_blocks, chosen, axis=0)
    partial_value = jnp.einsum(
        "snat,tnb->snab", gathered, value_blocks, preferred_element_type=jnp.float32
    )
    reduced = lax.psum_scatter(
        partial_value.reshape(lax.axis_size("ctx") * row_share, column_blocks, BLK * BLK),
        "ctx",
        scatter_dimension=0,
        tiled=True,
    )
    value_grad = lax.psum(reduced, "dp")
    return (query_grad, key_grad, value_grad)


def solution(mesh):
    in_specs = (
        P(None, ("dp", "ctx")),
        P("tensor", ("dp", "ctx")),
        P("tensor", ("dp", "ctx")),
        P(("dp", "ctx"), "tensor"),
        P(("dp", "ctx"), "tensor"),
        P(("dp", "ctx"), "tensor"),
        P(("dp", "ctx"), "tensor"),
        P("tensor", ("dp", "ctx")),
        P("tensor", None),
    )
    out_specs = (P(("dp", "ctx"), "tensor"), P(("dp", "ctx"), "tensor"), P("ctx", "tensor", None))
    return jax.shard_map(
        per_device, mesh=mesh, in_specs=in_specs, out_specs=out_specs, check_vma=False
    )
```

profile of v0, /device:TPU:1, one launch (start us, length us, event | category | flops | bytes accessed | tf_op | source)
XLA Modules:
  0.0 712.7 jit_solution(3989834290211773359)
XLA Ops:
  12.6 34.4 %while.72 = (s32[]{:T(128)}, bf16[8,256,256]{1,2,0:T(8,128)(2,1)}, f32[8,256,128]{2,1,0:T(8,128)}, f32[8,256]{1,0:T(8,128)S(1)}, f32[8]{0:T(128)S(1)}, /*index=5...) while((s32[]{:T(128)}, bf16[8,256,256]{1,2,0:T(8,128)(2,1)}, ...), condition=%wide.region_5.6_spmd, body=%wide.region_2.5_spmd.sunk | while | flops 84574080 | bytes 1523417 | solution.py:172
  48.0 2.0 copy.48
  51.6 39.0 %all-reduce = f32[128]{0:T(128)S(1)} all-reduce(f32[128]{0:T(128)S(1)} %dynamic-update-slice), channel_id=2, replica_groups=mesh['dp'=2,'ctx'=16,'tensor'=8] {'ctx'}, use_global_device_ids=true, to_apply=%add | all-reduce | flops 128 | bytes 1024
  90.6 29.6 %all-gather.2 = f32[128,128]{1,0:T(8,128)S(1)} all-gather(f32[8,128]{1,0:T(8,128)S(1)} %get-tuple-element.456), channel_id=4, replica_groups=mesh['dp'=2,'ctx'=16,'tensor'=8] {'ctx'}, dimensions={0}, use_global_device_ids=true | all-gather | bytes 69632 | tf_op jit(solution)/shard_map/all_gather | solution.py:15
  120.2 66.5 %all-gather.8.cloned.1.call-done = f32[128,128,128]{2,1,0:T(8,128)} async-done(((f32[8,128,128]{2,1,0:T(8,128)}), f32[128,128,128]{2,1,0:T(8,128)}) %all-gather.8.cloned.1.call-update) | async-done | bytes 8388624 | tf_op jit(solution)/shard_map/all_gather | solution.py:15
  186.7 20.1 %while.74 = (s32[]{:T(128)}, f32[8,128,128]{2,1,0:T(8,128)S(1)}, f32[8,128]{1,0:T(8,128)S(1)}, s32[]{:T(128)}, f32[16,8]{1,0:T(8,128)S(1)}, /*index=5*/f32[16,8,...) while((s32[]{:T(128)}, f32[8,128,128]{2,1,0:T(8,128)S(1)}, ...), condition=%wide.region_7.8_spmd.clone, body=%wide.region_6.7_spmd.clone.sunk | while | flops 528388 | bytes 1585415 | solution.py:28
  206.8 75.2 %while.73 = (s32[]{:T(128)}, f32[8,256,128]{1,2,0:T(8,128)}, f32[8,256,128]{1,2,0:T(8,128)}, f32[8,256,128]{1,2,0:T(8,128)}, f32[8,128,128]{2,1,0:T(8,128)S(1)},...) while((s32[]{:T(128)}, f32[8,256,128]{1,2,0:T(8,128)}, ...), condition=%wide.region_10.11_spmd, body=%wide.region_8.10_spmd.sunk | while | flops 220071168 | bytes 2862273 | solution.py:183
  222.5 1.8 fusion.181
  241.3 1.8 fusion.181
  260.1 1.8 fusion.181
  269.5 1.8 fusion.181
  278.9 1.8 fusion.181
  285.0 3.7 fusion.81
  288.7 10.9 %gather_fusion = bf16[256,64,256]{2,1,0:T(8,128)(2,1)} fusion(bf16[128,64,256]{2,1,0:T(8,128)(2,1)} %fusion.81, s32[1024]{0:T(1024)S(1)} %pad_clamp_fusion), kind=kCustom, calls=%fused_computation | custom fusion | bytes 16778240 | tf_op jit(solution)/shard_map/jit(_take)/gather | solution.py:222
  299.9 30.1 %all-gather.4 = f32[128,128]{1,0:T(8,128)S(1)} all-gather(f32[8,128]{1,0:T(8,128)S(1)} %get-tuple-element.464), channel_id=6, replica_groups=mesh['dp'=2,'ctx'=16,'tensor'=8] {'ctx'}, dimensions={0}, use_global_device_ids=true | all-gather | bytes 69632 | tf_op jit(solution)/shard_map/all_gather | solution.py:15
  330.0 84.7 %all-gather.10.cloned.1.call-done = f32[128,128,128]{2,1,0:T(8,128)} async-done(((f32[8,128,128]{2,1,0:T(8,128)}), f32[128,128,128]{2,1,0:T(8,128)}) %all-gather.10.cloned.1.call-update) | async-done | bytes 8388624 | tf_op jit(solution)/shard_map/all_gather | solution.py:15
  414.7 20.1 %while.75 = (s32[]{:T(128)}, f32[8,128,128]{2,1,0:T(8,128)S(1)}, f32[8,128]{1,0:T(8,128)S(1)}, s32[]{:T(128)}, f32[16,8,128,128]{3,2,1,0:T(8,128)}, /*index=5*/f...) while((s32[]{:T(128)}, f32[8,128,128]{2,1,0:T(8,128)S(1)}, ...), condition=%wide.region_12.13_spmd.clone, body=%wide.region_11.12_spmd.clone.sunk | while | flops 528392 | bytes 1585477 | solution.py:28
  435.5 8.6 %fusion.84 = f32[16,16,64,64]{2,3,0,1:T(8,128)} fusion(bf16[256,16,64,1]{0,2,3,1:T(8,128)(2,1)S(1)} %bitcast.307, bf16[16,16,64,256]{3,2,1,0:T(8,128)(2,1)} %bitcast.298, pred[16,16]{1,0:T(8,128)(4,1)S(1)} %copy.63), kind=kOutput, calls=%fused_computation.118 | convolution fusion | flops 541065216 | bytes 13107456 | tf_op jit(solution)/shard_map/snat,tnb->snab/dot_general | solution.py:223
  444.1 9.3 %copy.66 = f32[16,16,64,64]{3,2,1,0:T(8,128)} copy(f32[16,16,64,64]{2,3,0,1:T(8,128)} %fusion.84) | data formatting | bytes 8388608 | tf_op jit(solution)/shard_map/snat,tnb->snab/transpose | solution.py:223
  453.3 8.0 %reshape.163 = f32[16,16,4096]{2,1,0:T(8,128)} reshape(f32[16,16,64,64]{3,2,1,0:T(8,128)} %copy.66) | data formatting | bytes 8388608 | tf_op jit(solution)/shard_map/reshape | solution.py:227
  462.7 1.9 fusion.90
  464.9 200.6 %reduce-scatter.2.cloned.1.call-done = f32[1,16,4096]{2,1,0:T(8,128)} async-done(((f32[16,16,4096]{2,1,0:T(8,128)}), f32[1,16,4096]{2,1,0:T(8,128)}) %reduce-scatter.2.cloned.1.call-update) | async-done | bytes 262160 | tf_op jit(solution)/shard_map/reduce_scatter | solution.py:226
  665.5 2.7 multiply_convert_fusion
  668.2 36.3 %all-reduce.3.cloned.1.call-done = f32[1,16,4096]{2,1,0:T(8,128)} async-done(((f32[1,16,4096]{2,1,0:T(8,128)}), f32[1,16,4096]{2,1,0:T(8,128)}) %all-reduce.3.cloned.1.call-update) | async-done | bytes 262160 | tf_op jit(solution)/shard_map/psum | solution.py:232
  (367 shorter events, 148.7 us)
Async XLA Ops:
  7.2 179.5 %all-gather.8.cloned.1.call-start = ((), (), s32[]{:S(2)}) async-start(), calls=%async_computation.3 | async-start | bytes 8912896 | tf_op jit(solution)/shard_map/all_gather | solution.py:15
  10.1 39.9 %copy-start.6 = (u32[256]{0:T(256)S(1)}, u32[256]{0:T(256)}, u32[]{:S(2)}) copy-start(u32[256]{0:T(256)} %constant.157) | copy-start | bytes 3076
  47.0 0.8 copy-start
  47.9 366.9 %all-gather.10.cloned.1.call-start = ((), (), s32[]{:S(2)}) async-start(), calls=%async_computation.4 | async-start | bytes 8912896 | tf_op jit(solution)/shard_map/all_gather | solution.py:15
  206.8 76.2 %copy-start.5 = (s32[16,16]{1,0:T(8,128)S(1)}, s32[16,16]{1,0:T(8,128)}, u32[]{:S(2)}) copy-start(s32[16,16]{1,0:T(8,128)} %param.25) | copy-start | bytes 3076
  282.0 0.8 copy-start.1
  282.8 382.7 %reduce-scatter.2.cloned.1.call-start = ((), (), s32[]{:S(2)}) async-start(), calls=%async_computation.1 | async-start | bytes 4456448 | tf_op jit(solution)/shard_map/reduce_scatter | solution.py:226
  288.7 146.1 %copy-start.3 = (f32[8,256,128]{1,2,0:T(8,128)S(1)}, f32[8,256,128]{1,2,0:T(8,128)}, u32[]{:S(2)}) copy-start(f32[8,256,128]{1,2,0:T(8,128)} %get-tuple-element.467) | copy-start | bytes 3145732
  453.3 8.1 %copy-start.2 = (f32[8,256,128]{1,2,0:T(8,128)S(1)}, f32[8,256,128]{1,2,0:T(8,128)}, u32[]{:S(2)}) copy-start(f32[8,256,128]{1,2,0:T(8,128)} %get-tuple-element.461) | copy-start | bytes 3145732
  461.3 204.2 %copy-start.4 = (bf16[256,1024]{1,0:T(8,128)(2,1)S(1)}, bf16[256,1024]{1,0:T(8,128)(2,1)}, u32[]{:S(2)}) copy-start(bf16[256,1024]{1,0:T(8,128)(2,1)} %param.22) | copy-start | bytes 1572868
  461.4 243.2 %all-reduce.3.cloned.1.call-start = ((), (), s32[]{:S(2)}) async-start(), calls=%async_computation.2 | async-start | bytes 524288 | tf_op jit(solution)/shard_map/psum | solution.py:232
Sparse Core Ops, SparseCore 0:
  48.0 138.6 all-gather.7
  282.9 131.7 all-gather.9
  461.5 203.9 reduce-scatter.1
  667.9 36.5 all-reduce.2
where the time goes:
time: 717 us; the launch traced here: 713 us
  waiting for transfers between devices  388 us (54%)
  blocking collectives  98.6 us (14%)
  matrix products  92.2 us (13%)
  local copies, waits for them, and re-layouts  57.3 us (8%)
  other arithmetic  54.8 us (8%)
  between operations  14.8 us (2%)
    reduce_scatter x1, waiting for transfers between devices, per_device(): lax.psum_scatter(partial_value.reshape(lax.axis_size('ctx') * row_share,...  201 us
    all_gather x2, waiting for transfers between devices, entering(): everything = jax.tree.map(lambda part: lax.all_gather(part, axis), value)  151 us
    all_gather x2, blocking collectives, entering(): everything = jax.tree.map(lambda part: lax.all_gather(part, axis), value)  59.7 us
    select_n x64, other arithmetic, turn(): return jax.tree.map(lambda a, b: jnp.where(reached, a, b), new, before)  39.8 us
    unnamed x1, blocking collectives  39 us
    psum x1, waiting for transfers between devices, per_device(): value_grad = lax.psum(reduced, 'dp')  36.3 us
  transfers between devices with their start and end apart: 4, of which 4 were waited for; matrix products, arithmetic and copies ran while one was open for 4% of the time, Pallas kernels for 0%

commit v1 on v0

--- a/solution.py
+++ b/solution.py
@@ -1,3 +1,4 @@
+import functools
 import jax
 import jax.numpy as jnp
 from jax import lax
@@ -8,6 +9,13 @@
 BLK = 64
 SEL = 16
 highest = lax.Precision.HIGHEST
+
+
+def pack_spots(shard_in, along_axis):
+    return jnp.sum(lax.all_gather(shard_in, along_axis), axis=0)
+
+
+_hold_islands = functools.partial(pack_spots, along_axis="dp")
 
 
 def entering(value, axis, combine, identity, reverse):
@@ -229,7 +237,7 @@
         scatter_dimension=0,
         tiled=True,
     )
-    value_grad = lax.psum(reduced, "dp")
+    value_grad = _hold_islands(reduced)
     return (query_grad, key_grad, value_grad)
 
 

time: 717 us -> 687 us (0.958)
  waiting for transfers between devices: 388 us -> 350 us
    psum x1 -> x0, waiting for transfers between devices: 36.3 us -> none  [per_device(): value_grad = lax.psum(reduced, 'dp')]
  transfers between devices with their start and end apart: 4 -> 3, of which waited for: 4 -> 3; matrix products, arithmetic and copies ran while one was open for 4% -> 4% of each run, Pallas kernels for 0% -> 0%
where the time goes in v1:
time: 687 us; the launch traced here: 679 us
  waiting for transfers between devices  350 us (51%)
  blocking collectives  105 us (15%)
  matrix products  91.9 us (13%)
  local copies, waits for them, and re-layouts  55.6 us (8%)
  other arithmetic  55.5 us (8%)
  between operations  14.6 us (2%)
    reduce_scatter x1, waiting for transfers between devices, per_device(): lax.psum_scatter(partial_value.reshape(lax.axis_size('ctx') * row_share,...  198 us
    all_gather x2, waiting for transfers between devices, entering(): everything = jax.tree.map(lambda part: lax.all_gather(part, axis), value)  152 us
    all_gather x2, blocking collectives, entering(): everything = jax.tree.map(lambda part: lax.all_gather(part, axis), value)  59.5 us
    select_n x64, other arithmetic, turn(): return jax.tree.map(lambda a, b: jnp.where(reached, a, b), new, before)  39.8 us
    unnamed x1, blocking collectives  38.9 us
    dot_general x8, matrix products, second_phase(): lax.dot_general(weights_low, scaled_low, dims_of(0, 0), preferred_element...  14 us
  transfers between devices with their start and end apart: 3, of which 3 were waited for; matrix products, arithmetic and copies ran while one was open for 4% of the time, Pallas kernels for 0%

profile of v1, /device:TPU:1, one launch (start us, length us, event | category | flops | bytes accessed | tf_op | source)
XLA Modules:
  0.0 678.6 jit_solution(14177343074194215215)
XLA Ops:
  12.6 34.3 %while.72 = (s32[]{:T(128)}, bf16[8,256,256]{1,2,0:T(8,128)(2,1)}, f32[8,256,128]{2,1,0:T(8,128)}, f32[8,256]{1,0:T(8,128)S(1)}, f32[8]{0:T(128)S(1)}, /*index=5...) while((s32[]{:T(128)}, bf16[8,256,256]{1,2,0:T(8,128)(2,1)}, ...), condition=%wide.region_5.6_spmd, body=%wide.region_2.5_spmd.sunk | while | flops 84574080 | bytes 1523417 | solution.py:180
  47.8 2.0 copy.48
  51.3 38.9 %all-reduce = f32[128]{0:T(128)S(1)} all-reduce(f32[128]{0:T(128)S(1)} %dynamic-update-slice), channel_id=2, replica_groups=mesh['dp'=2,'ctx'=16,'tensor'=8] {'ctx'}, use_global_device_ids=true, to_apply=%add | all-reduce | flops 128 | bytes 1024
  90.2 29.2 %all-gather.2 = f32[128,128]{1,0:T(8,128)S(1)} all-gather(f32[8,128]{1,0:T(8,128)S(1)} %get-tuple-element.456), channel_id=4, replica_groups=mesh['dp'=2,'ctx'=16,'tensor'=8] {'ctx'}, dimensions={0}, use_global_device_ids=true | all-gather | bytes 69632 | tf_op jit(solution)/shard_map/all_gather | solution.py:23
  119.4 67.1 %all-gather.9.cloned.1.call-done = f32[128,128,128]{2,1,0:T(8,128)} async-done(((f32[8,128,128]{2,1,0:T(8,128)}), f32[128,128,128]{2,1,0:T(8,128)}) %all-gather.9.cloned.1.call-update) | async-done | bytes 8388624 | tf_op jit(solution)/shard_map/all_gather | solution.py:23
  186.5 20.1 %while.74 = (s32[]{:T(128)}, f32[8,128,128]{2,1,0:T(8,128)S(1)}, f32[8,128]{1,0:T(8,128)S(1)}, s32[]{:T(128)}, f32[16,8]{1,0:T(8,128)S(1)}, /*index=5*/f32[16,8,...) while((s32[]{:T(128)}, f32[8,128,128]{2,1,0:T(8,128)S(1)}, ...), condition=%wide.region_7.8_spmd.clone, body=%wide.region_6.7_spmd.clone.sunk | while | flops 528388 | bytes 1585415 | solution.py:36
  206.6 75.0 %while.73 = (s32[]{:T(128)}, f32[8,256,128]{1,2,0:T(8,128)}, f32[8,256,128]{1,2,0:T(8,128)}, f32[8,256,128]{1,2,0:T(8,128)}, f32[8,128,128]{2,1,0:T(8,128)S(1)},...) while((s32[]{:T(128)}, f32[8,256,128]{1,2,0:T(8,128)}, ...), condition=%wide.region_10.11_spmd, body=%wide.region_8.10_spmd.sunk | while | flops 220071168 | bytes 2862273 | solution.py:191
  222.2 1.8 fusion.181
  231.6 1.8 fusion.181
  250.4 1.8 fusion.181
  259.8 1.8 fusion.181
  278.5 1.8 fusion.181
  284.6 3.7 fusion.81
  288.3 10.9 %gather_fusion = bf16[256,64,256]{2,1,0:T(8,128)(2,1)} fusion(bf16[128,64,256]{2,1,0:T(8,128)(2,1)} %fusion.81, s32[1024]{0:T(1024)S(1)} %pad_clamp_fusion), kind=kCustom, calls=%fused_computation | custom fusion | bytes 16778240 | tf_op jit(solution)/shard_map/jit(_take)/gather | solution.py:230
  299.5 30.4 %all-gather.4 = f32[128,128]{1,0:T(8,128)S(1)} all-gather(f32[8,128]{1,0:T(8,128)S(1)} %get-tuple-element.464), channel_id=6, replica_groups=mesh['dp'=2,'ctx'=16,'tensor'=8] {'ctx'}, dimensions={0}, use_global_device_ids=true | all-gather | bytes 69632 | tf_op jit(solution)/shard_map/all_gather | solution.py:23
  329.9 84.6 %all-gather.11.cloned.1.call-done = f32[128,128,128]{2,1,0:T(8,128)} async-done(((f32[8,128,128]{2,1,0:T(8,128)}), f32[128,128,128]{2,1,0:T(8,128)}) %all-gather.11.cloned.1.call-update) | async-done | bytes 8388624 | tf_op jit(solution)/shard_map/all_gather | solution.py:23
  414.5 20.1 %while.75 = (s32[]{:T(128)}, f32[8,128,128]{2,1,0:T(8,128)S(1)}, f32[8,128]{1,0:T(8,128)S(1)}, s32[]{:T(128)}, f32[16,8,128,128]{3,2,1,0:T(8,128)}, /*index=5*/f...) while((s32[]{:T(128)}, f32[8,128,128]{2,1,0:T(8,128)S(1)}, ...), condition=%wide.region_12.13_spmd.clone, body=%wide.region_11.12_spmd.clone.sunk | while | flops 528392 | bytes 1585477 | solution.py:36
  435.2 8.6 %fusion.84 = f32[16,16,64,64]{2,3,0,1:T(8,128)} fusion(bf16[256,16,64,1]{0,2,3,1:T(8,128)(2,1)S(1)} %bitcast.308, bf16[16,16,64,256]{3,2,1,0:T(8,128)(2,1)} %bitcast.299, pred[16,16]{1,0:T(8,128)(4,1)S(1)} %copy.63), kind=kOutput, calls=%fused_computation.118 | convolution fusion | flops 541065216 | bytes 13107456 | tf_op jit(solution)/shard_map/snat,tnb->snab/dot_general | solution.py:231
  443.8 9.3 %copy.66 = f32[16,16,64,64]{3,2,1,0:T(8,128)} copy(f32[16,16,64,64]{2,3,0,1:T(8,128)} %fusion.84) | data formatting | bytes 8388608 | tf_op jit(solution)/shard_map/snat,tnb->snab/transpose | solution.py:231
  453.1 8.0 %reshape.164 = f32[16,16,4096]{2,1,0:T(8,128)} reshape(f32[16,16,64,64]{3,2,1,0:T(8,128)} %copy.66) | data formatting | bytes 8388608 | tf_op jit(solution)/shard_map/reshape | solution.py:235
  462.4 1.8 fusion.90
  464.6 2.7 multiply_convert_fusion
  467.3 198.0 %reduce-scatter.2.cloned.1.call-done = f32[1,16,4096]{2,1,0:T(8,128)} async-done(((f32[16,16,4096]{2,1,0:T(8,128)}), f32[1,16,4096]{2,1,0:T(8,128)}) %reduce-scatter.2.cloned.1.call-update) | async-done | bytes 262160 | tf_op jit(solution)/shard_map/reduce_scatter | solution.py:234
  665.3 6.1 all-gather.5
  (365 shorter events, 147.3 us)
Async XLA Ops:
  7.2 179.3 %all-gather.9.cloned.1.call-start = ((), (), s32[]{:S(2)}) async-start(), calls=%async_computation.2 | async-start | bytes 8912896 | tf_op jit(solution)/shard_map/all_gather | solution.py:23
  10.1 39.8 %copy-start.6 = (u32[256]{0:T(256)S(1)}, u32[256]{0:T(256)}, u32[]{:S(2)}) copy-start(u32[256]{0:T(256)} %constant.158) | copy-start | bytes 3076
  46.9 0.8 copy-start
  47.7 366.7 %all-gather.11.cloned.1.call-start = ((), (), s32[]{:S(2)}) async-start(), calls=%async_computation.3 | async-start | bytes 8912896 | tf_op jit(solution)/shard_map/all_gather | solution.py:23
  206.6 76.0 %copy-start.5 = (s32[16,16]{1,0:T(8,128)S(1)}, s32[16,16]{1,0:T(8,128)}, u32[]{:S(2)}) copy-start(s32[16,16]{1,0:T(8,128)} %param.25) | copy-start | bytes 3076
  281.6 0.8 copy-start.1
  282.4 382.9 %reduce-scatter.2.cloned.1.call-start = ((), (), s32[]{:S(2)}) async-start(), calls=%async_computation.1 | async-start | bytes 4456448 | tf_op jit(solution)/shard_map/reduce_scatter | solution.py:234
  288.3 146.2 %copy-start.3 = (f32[8,256,128]{1,2,0:T(8,128)S(1)}, f32[8,256,128]{1,2,0:T(8,128)}, u32[]{:S(2)}) copy-start(f32[8,256,128]{1,2,0:T(8,128)} %get-tuple-element.467) | copy-start | bytes 3145732
  453.1 8.0 %copy-start.2 = (f32[8,256,128]{1,2,0:T(8,128)S(1)}, f32[8,256,128]{1,2,0:T(8,128)}, u32[]{:S(2)}) copy-start(f32[8,256,128]{1,2,0:T(8,128)} %get-tuple-element.461) | copy-start | bytes 3145732
  461.1 3.6 copy-start.4
Sparse Core Ops, SparseCore 0:
  47.9 138.5 all-gather.8
  282.5 131.8 all-gather.10
  461.2 204.0 reduce-scatter.1
